TPU v7x, 32 devices: a whole 2x2x4 slice. The times are simulated.
32 devices in a mesh: grp: 2 (over x), tok: 4 (over y, core), feat: 4 (over z).
Axes of the slice: x: 2, y: 2, z: 4, core: 2. Of those that a mesh axis runs over, the one named last changes fastest.
Arguments:
- activations: bfloat16 [4096, 3072], P(('grp', 'tok', 'feat')), parts along dimension 0, may hold values from -6 to 6
- block_lists: int32 [2048, 4], P(('grp', 'tok', 'feat')), parts along dimension 0, may hold values from 0 to 15, as said below
- top_positions: int32 [4096, 64], P(('grp', 'tok', 'feat')), parts along dimension 0, may hold values from 0 to 2047, as said below
- enc_weight: bfloat16 [3072, 8192], P(None, ('tok', 'feat')), may hold values from -0.109375 to 0.109375
- enc_bias: float32 [8192], P(('tok', 'feat')), may hold values from -3 to 3
- dec_weight: bfloat16 [8192, 3072], P(('tok', 'feat')), may hold values from -2.5 to 2.5
- dec_bias: float32 [3072], replicated, may hold values from -6 to 6
Outputs:
- enc_grad: bfloat16 [3072, 16384], P(None, ('grp', 'tok', 'feat')), parts along dimension 1
- dec_grad: bfloat16 [16384, 3072], P(('grp', 'tok', 'feat')), parts along dimension 0
There are 2 independent parts, one for each index of `grp`. A program takes and returns all parts, laid end to end along the dimension named above; an argument that names none is the same for every part. Nothing has to cross between parts.
Inputs may be any that keep to these rules, and one draw needn't show every extreme that they name: `block_lists`: each row block names 4 different feature blocks. In the aligned blocks of 64 rows that one device holds, no feature block is named more than 24 times. In every draw one feature block is named exactly 24 times in every such block of rows. `top_positions`: the 64 entries of a token are distinct.
All inputs are finite; a program needn't handle non-finite values.
Results may differ from a plain program's by a relative error of at most 0.0058.
Values may be sent and summed in bfloat16 or wider, within the bound.
A program may use at most 128 MiB of HBM per device.

v0:
```python
import jax
import jax.numpy as jnp
from jax import lax
from jax.sharding import PartitionSpec as P


def dispatch_rows(send_x, send_rel):
    result = (
        lax.all_to_all(send_x, ("tok", "feat"), split_axis=0, concat_axis=0, tiled=True),
        lax.all_to_all(send_rel, ("tok", "feat"), split_axis=0, concat_axis=0, tiled=True),
    )
    return result


def return_partials(partial_value):
    result = lax.all_to_all(partial_value, ("tok", "feat"), split_axis=0, concat_axis=0, tiled=True)
    return result


def dispatch_errors(send_err):
    result = lax.all_to_all(send_err, ("tok", "feat"), split_axis=0, concat_axis=0, tiled=True)
    return result


def on_device(activations, block_lists, top_positions, enc_weight, enc_bias, dec_weight, dec_bias):
    owner_count = lax.axis_size(("tok", "feat"))
    token_count, model_width = activations.shape
    block_rows, active_count = block_lists.shape
    group_rows = token_count // block_rows
    feat_block = enc_weight.shape[1]
    top_count = top_positions.shape[1]
    slot_count = max(2, 3 * token_count * active_count // (2 * group_rows * owner_count))
    per_owner = slot_count * group_rows
    buffer_rows = owner_count * per_owner
    pair_count = block_rows * active_count
    pair_ids = block_lists.reshape(pair_count)
    pair_order = jnp.arange(pair_count, dtype=jnp.int32)
    earlier = (pair_ids[:, None] == pair_ids[None, :]) & (pair_order[None, :] < pair_order[:, None])
    pair_rank = jnp.sum(earlier.astype(jnp.int32), axis=1)
    lane_index = jnp.arange(group_rows, dtype=jnp.int32)
    target = (
        (pair_ids * per_owner + pair_rank * group_rows)[:, None] + lane_index[None, :]
    ).reshape(-1)
    source = ((pair_order // active_count * group_rows)[:, None] + lane_index[None, :]).reshape(-1)
    column = jnp.repeat(pair_order % active_count, group_rows)
    slot_index = jnp.arange(buffer_rows, dtype=jnp.int32)
    hit_bool = slot_index[:, None] == target[None, :]
    hit_float = hit_bool.astype(jnp.float32)
    place_float = jnp.sum(
        hit_float.reshape(buffer_rows, block_rows, active_count, group_rows), axis=2
    ).reshape(buffer_rows, token_count)
    place = place_float.astype(jnp.bfloat16)
    filled = jnp.sum(place_float, axis=1)
    send_x = jnp.dot(place, activations, preferred_element_type=jnp.float32).astype(jnp.bfloat16)
    offsets = top_positions[source] - column[:, None] * feat_block
    offsets = jnp.where((offsets >= 0) & (offsets < feat_block), offsets, feat_block)
    rel_float = (
        jnp.dot(hit_float, offsets.astype(jnp.float32), precision=lax.Precision.HIGHEST)
        + (1.0 - filled)[:, None] * feat_block
    )
    send_rel = rel_float.astype(jnp.int32)
    recv_x, recv_rel = dispatch_rows(
        send_x.reshape(owner_count, per_owner, model_width),
        send_rel.reshape(owner_count, per_owner, top_count),
    )
    recv_x = recv_x.reshape(buffer_rows, model_width)
    recv_rel = recv_rel.reshape(buffer_rows, top_count)
    feature_iota = jnp.arange(feat_block, dtype=jnp.int32)
    mask_bool = jnp.zeros((buffer_rows, feat_block), jnp.bool_)
    for begin in range(0, top_count, 8):
        piece = recv_rel[:, begin : begin + 8]
        mask_bool = mask_bool | jnp.any(piece[:, :, None] == feature_iota[None, None, :], axis=1)
    feat_mask = mask_bool.astype(jnp.float32)
    pre_acts = jnp.dot(recv_x, enc_weight, preferred_element_type=jnp.float32) + enc_bias
    code_vals = (feat_mask * pre_acts).astype(jnp.bfloat16)
    partial_value = jnp.dot(code_vals, dec_weight, preferred_element_type=jnp.float32).astype(
        jnp.bfloat16
    )
    returned = return_partials(partial_value.reshape(owner_count, per_owner, model_width)).reshape(
        buffer_rows, model_width
    )
    summed = lax.dot_general(
        place, returned, (((0,), (0,)), ((), ())), preferred_element_type=jnp.float32
    )
    residual = (summed + dec_bias - activations.astype(jnp.float32)).astype(jnp.bfloat16)
    send_err = jnp.dot(place, residual, preferred_element_type=jnp.float32).astype(jnp.bfloat16)
    recv_err = dispatch_errors(send_err.reshape(owner_count, per_owner, model_width)).reshape(
        buffer_rows, model_width
    )
    grad_codes = lax.dot_general(
        recv_err, dec_weight, (((1,), (1,)), ((), ())), preferred_element_type=jnp.float32
    )
    grad_pre = (feat_mask * grad_codes).astype(jnp.bfloat16)
    enc_grad = lax.dot_general(
        recv_x, grad_pre, (((0,), (0,)), ((), ())), preferred_element_type=jnp.float32
    ).astype(jnp.bfloat16)
    raw_grad = lax.dot_general(
        code_vals, recv_err, (((0,), (0,)), ((), ())), preferred_element_type=jnp.float32
    )
    dec_float = dec_weight.astype(jnp.float32)
    along_coef = jnp.sum(raw_grad * dec_float, axis=1) / (
        jnp.sum(dec_float * dec_float, axis=1) + 1e-06
    )
    dec_grad = (raw_grad - along_coef[:, None] * dec_float).astype(jnp.bfloat16)
    return (enc_grad, dec_grad)


def solution(mesh):
    placed = (
        P(("grp", "tok", "feat"), None),
        P(("grp", "tok", "feat"), None),
        P(("grp", "tok", "feat"), None),
        P(None, ("tok", "feat")),
        P(("tok", "feat")),
        P(("tok", "feat"), None),
        P(),
    )
    return jax.shard_map(
        on_device,
        mesh=mesh,
        in_specs=placed,
        out_specs=(P(None, ("grp", "tok", "feat")), P(("grp", "tok", "feat"), None)),
        check_vma=False,
    )
```

profile of v0, /device:TPU:0, one launch (start us, length us, event | category | flops | bytes accessed | tf_op | source)
XLA Modules:
  0.0 386.0 jit_solution(7723366868025504565)
XLA Ops:
  5.4 1.0 gather_fusion
  6.4 1.6 fusion.16
  8.0 1.1 copy.75
  10.0 7.4 %all-to-all-start.1 = ((s32[16,1,3072]{2,1,0:T(1,128)}), s32[16,1,3072]{2,1,0:T(1,128)S(1)}, u32[]{:S(2)}, u32[]{:S(2)}) async-start(s32[16,1,3072]{2,1,0:T(1,128)} %reshape.174), calls=%async_computation.1 | async-start | bytes 393216 | tf_op jit(solution)/shard_map/all_to_all | solution.py:10
  17.4 1.8 copy.63
  19.2 1.0 convert_element_type.60
  20.2 4.8 %convolution_convert_fusion.2 = bf16[768,3072]{1,0:T(8,128)(2,1)} fusion(bf16[768,128]{0,1:T(8,128)(2,1)S(1)} %convert_element_type.60, bf16[128,3072]{1,0:T(8,128)(2,1)} %param.7), kind=kOutput, calls=%fused_computation.26 | convolution fusion | flops 606339072 | bytes 5701632 | tf_op jit(solution)/shard_map/dot_general | solution.py:54
  25.5 5.5 %all-to-all-start = ((bf16[16,48,3072]{2,1,0:T(8,128)(2,1)}), bf16[16,48,3072]{2,1,0:T(8,128)(2,1)}, u32[]{:S(2)}, u32[]{:S(2)}) async-start(bf16[16,48,3072]{2,1,0:T(8,128)(2,1)} %bitcast.26), calls=%async_computation | async-start | bytes 9437184 | tf_op jit(solution)/shard_map/all_to_all | solution.py:9
  31.6 1.8 reduce.2
  33.4 1.0 reshape.175
  35.2 8.7 %fusion = (pred[768,512]{1,0:T(8,128)(4,1)S(1)}, pred[768,512]{1,0:T(8,128)(4,1)S(1)}) fusion(s32[768,8]{1,0:T(8,128)S(1)} %get-tuple-element.12, s32[768,8]{1,0:T(8,128)S(1)} %get-tuple-element.6), kind=kLoop, calls=%fused_computation.9 | loop fusion | flops 11796480 | bytes 835584 | tf_op jit(solution)/shard_map/reduce_or | solution.py:72
  43.9 8.7 %fusion.6 = (pred[768,512]{1,0:T(8,128)(4,1)S(1)}, pred[768,512]{1,0:T(8,128)(4,1)S(1)}) fusion(s32[768,8]{1,0:T(8,128)S(1)} %get-tuple-element.7, s32[768,8]{1,0:T(8,128)S(1)} %get-tuple-element.13), kind=kLoop, calls=%fused_computation.15 | loop fusion | flops 11796480 | bytes 835584 | tf_op jit(solution)/shard_map/reduce_or | solution.py:72
  52.6 8.7 %fusion.4 = (pred[768,512]{1,0:T(8,128)(4,1)S(1)}, pred[768,512]{1,0:T(8,128)(4,1)S(1)}) fusion(s32[768,8]{1,0:T(8,128)S(1)} %get-tuple-element.9, s32[768,8]{1,0:T(8,128)S(1)} %get-tuple-element.8), kind=kLoop, calls=%fused_computation.13 | loop fusion | flops 11796480 | bytes 835584 | tf_op jit(solution)/shard_map/reduce_or | solution.py:72
  61.2 8.7 %fusion.2 = (pred[768,512]{1,0:T(8,128)(4,1)S(1)}, pred[768,512]{1,0:T(8,128)(4,1)S(1)}) fusion(s32[768,8]{1,0:T(8,128)S(1)} %get-tuple-element.11, s32[768,8]{1,0:T(8,128)S(1)} %get-tuple-element.10), kind=kLoop, calls=%fused_computation.11 | loop fusion | flops 11796480 | bytes 835584 | tf_op jit(solution)/shard_map/reduce_or | solution.py:72
  70.8 65.9 %all-to-all-done = bf16[16,48,3072]{2,1,0:T(8,128)(2,1)} async-done(((bf16[16,48,3072]{2,1,0:T(8,128)(2,1)}), bf16[16,48,3072]{2,1,0:T(8,128)(2,1)}, u32[]{:S(2)}, u32[]{:S(2)}) %all-to-all-start) | async-done | bytes 4718624 | tf_op jit(solution)/shard_map/all_to_all | solution.py:9
  136.7 5.1 %select_convert_fusion.1 = bf16[768,512]{1,0:T(8,128)(2,1)S(1)} fusion(pred[768,512]{1,0:T(32,128)(4,1)S(1)} %or_or_fusion, bf16[768,3072]{1,0:T(8,128)(2,1)} %bitcast.1, bf16[3072,512]{1,0:T(8,128)(2,1)S(1)} %copy-done, f32[512]{0:T(512)S(1)} %copy-done.10), kind=kOutput, calls=%fused_computation.34 | convolution fusion | flops 2417098752 | bytes 9046016 | tf_op jit(solution)/shard_map/dot_general | solution.py:74
  141.9 2.8 convolution_convert_fusion.1
  144.7 109.2 %all_to_all.20 = bf16[16,48,3072]{2,1,0:T(8,128)(2,1)} all-to-all(bf16[16,48,3072]{2,1,0:T(8,128)(2,1)S(1)} %bitcast.32), channel_id=1, replica_groups=mesh['grp'=2,'tok'=4,'feat'=4] {'tok','feat'}, dimensions={0} | all-to-all | bytes 9437184 | tf_op jit(solution)/shard_map/all_to_all | solution.py:16
  254.0 6.9 %convolution_convert_fusion = bf16[768,3072]{1,0:T(8,128)(2,1)} fusion(bf16[768,128]{0,1:T(8,128)(2,1)S(1)} %copy-done.4, bf16[768,3072]{1,0:T(8,128)(2,1)} %bitcast.30, bf16[128,3072]{1,0:T(8,128)(2,1)} %param.7, f32[3072]{0:T(1024)S(1)} %copy-done.9), kind=kOutput, calls=%fused_computation.24 | convolution fusion | flops 1211891712 | bytes 10432512 | tf_op jit(solution)/shard_map/dot_general | solution.py:86
  260.8 109.7 %all_to_all.21 = bf16[16,48,3072]{2,1,0:T(8,128)(2,1)S(1)} all-to-all(bf16[16,48,3072]{2,1,0:T(8,128)(2,1)} %bitcast.31), channel_id=1, replica_groups=mesh['grp'=2,'tok'=4,'feat'=4] {'tok','feat'}, dimensions={0} | all-to-all | bytes 9437184 | tf_op jit(solution)/shard_map/all_to_all | solution.py:21
  370.5 2.6 select_convert_fusion
  373.2 3.3 fusion.9
  376.5 6.4 %convolution_convert_fusion.3 = bf16[3072,512]{1,0:T(8,128)(2,1)} fusion(bf16[768,3072]{1,0:T(8,128)(2,1)} %bitcast.1, bf16[768,512]{1,0:T(8,128)(2,1)S(1)} %select_convert_fusion), kind=kOutput, calls=%fused_computation.27 | convolution fusion | flops 2417491968 | bytes 8650752 | tf_op jit(solution)/shard_map/dot_general | solution.py:94
  382.9 3.1 fusion.11
  (49 shorter events, 8.3 us)
Async XLA Ops:
  0.6 136.1 %copy-start = (bf16[3072,512]{1,0:T(8,128)(2,1)S(1)}, bf16[3072,512]{1,0:T(8,128)(2,1)}, u32[]{:S(2)}) copy-start(bf16[3072,512]{1,0:T(8,128)(2,1)} %param.10) | copy-start | bytes 9437188
  10.0 15.5 %all-to-all-start.1 = ((s32[16,1,3072]{2,1,0:T(1,128)}), s32[16,1,3072]{2,1,0:T(1,128)S(1)}, u32[]{:S(2)}, u32[]{:S(2)}) async-start(s32[16,1,3072]{2,1,0:T(1,128)} %reshape.174), calls=%async_computation.1 | async-start | bytes 393216 | tf_op jit(solution)/shard_map/all_to_all | solution.py:10
  20.2 5.3 %copy-start.3 = (bf16[768,128]{0,1:T(8,128)(2,1)}, bf16[768,128]{0,1:T(8,128)(2,1)S(1)}, u32[]{:S(2)}) copy-start(bf16[768,128]{0,1:T(8,128)(2,1)S(1)} %convert_element_type.60) | copy-start | bytes 589828
  25.5 111.2 %all-to-all-start = ((bf16[16,48,3072]{2,1,0:T(8,128)(2,1)}), bf16[16,48,3072]{2,1,0:T(8,128)(2,1)}, u32[]{:S(2)}, u32[]{:S(2)}) async-start(bf16[16,48,3072]{2,1,0:T(8,128)(2,1)} %bitcast.26), calls=%async_computation | async-start | bytes 9437184 | tf_op jit(solution)/shard_map/all_to_all | solution.py:9
  35.2 101.5 %copy-start.10 = (f32[512]{0:T(512)S(1)}, f32[512]{0:T(512)}, u32[]{:S(2)}) copy-start(f32[512]{0:T(512)} %param.11) | copy-start | bytes 6148
  70.8 71.1 %copy-start.7 = (pred[768,512]{1,0:T(32,128)(4,1)}, pred[768,512]{1,0:T(32,128)(4,1)S(1)}, u32[]{:S(2)}) copy-start(pred[768,512]{1,0:T(32,128)(4,1)S(1)} %or_or_fusion) | copy-start | bytes 1179652
  136.7 5.1 %copy-start.1 = (bf16[512,3072]{1,0:T(8,128)(2,1)S(1)}, bf16[512,3072]{1,0:T(8,128)(2,1)}, u32[]{:S(2)}) copy-start(bf16[512,3072]{1,0:T(8,128)(2,1)} %param.12) | copy-start | bytes 9437188
  141.9 2.8 copy-start.5
  144.7 109.2 %copy-start.4 = (bf16[768,128]{0,1:T(8,128)(2,1)S(1)}, bf16[768,128]{0,1:T(8,128)(2,1)}, u32[]{:S(2)}) copy-start(bf16[768,128]{0,1:T(8,128)(2,1)} %copy-done.3) | copy-start | bytes 589828
  144.7 109.2 %copy-start.9 = (f32[3072]{0:T(1024)S(1)}, f32[3072]{0:T(1024)}, u32[]{:S(2)}) copy-start(f32[3072]{0:T(1024)} %param.13) | copy-start | bytes 36868
  260.8 109.7 %copy-start.2 = (bf16[512,3072]{1,0:T(8,128)(2,1)S(1)}, bf16[512,3072]{1,0:T(8,128)(2,1)}, u32[]{:S(2)}) copy-start(bf16[512,3072]{1,0:T(8,128)(2,1)} %param.12) | copy-start | bytes 9437188
  260.8 109.7 %copy-start.8 = (pred[768,512]{1,0:T(32,128)(4,1)S(1)}, pred[768,512]{1,0:T(32,128)(4,1)}, u32[]{:S(2)}) copy-start(pred[768,512]{1,0:T(32,128)(4,1)} %copy-done.7) | copy-start | bytes 1179652
  370.5 2.6 copy-start.6
where the time goes:
time: 387 us; the launch traced here: 386 us
  blocking collectives  219 us (57%)
  waiting for transfers between devices  66.5 us (17%)
  other arithmetic  42.5 us (11%)
  matrix products  33.5 us (9%)
  starting transfers between devices  12.9 us (3%)
  local copies, waits for them, and re-layouts  10.8 us (3%)
    all_to_all x1, blocking collectives, dispatch_errors(): lax.all_to_all(send_err, ('tok', 'feat'), split_axis=0, concat_axis=0, ti...  110 us
    all_to_all x1, blocking collectives, return_partials(): lax.all_to_all(partial_value, ('tok', 'feat'), split_axis=0, concat_axis=...  109 us
    all_to_all x1, waiting for transfers between devices, dispatch_rows(): lax.all_to_all(send_x, ('tok', 'feat'), split_axis=0, concat_axis=0, tile...  65.9 us
    reduce_or x4, other arithmetic, on_device(): jnp.any(piece[:, :, None] == feature_iota[None, None, :], axis=1)  34.7 us
  transfers between devices with their start and end apart: 2, of which 2 were waited for; matrix products, arithmetic and copies ran while one was open for 12% of the time, Pallas kernels for 0%

commit v1 on v0

--- a/solution.py
+++ b/solution.py
@@ -22,7 +22,7 @@
     return result
 
 
-def on_device(activations, block_lists, top_positions, enc_weight, enc_bias, dec_weight, dec_bias):
+def routed_plan(activations, block_lists, top_positions, enc_weight, enc_bias, dec_weight, dec_bias):
     owner_count = lax.axis_size(("tok", "feat"))
     token_count, model_width = activations.shape
     block_rows, active_count = block_lists.shape
@@ -105,6 +105,80 @@
     return (enc_grad, dec_grad)
 
 
+GROUP = ("tok", "feat")
+
+
+def global_ids(block_lists, top_positions, feat_block):
+    token_count = top_positions.shape[0]
+    block_rows, active_count = block_lists.shape
+    lists = jnp.repeat(block_lists, token_count // block_rows, axis=0)
+    column = top_positions // feat_block
+    chosen = jnp.zeros_like(top_positions)
+    for k in range(active_count):
+        chosen = jnp.where(column == k, lists[:, k : k + 1], chosen)
+    return chosen * feat_block + top_positions % feat_block
+
+
+def select_mask(rel, feat_block):
+    words = feat_block // 8
+    inside = (rel >= 0) & (rel < feat_block)
+    word = jnp.where(inside, rel // 8, words)
+    bit = jnp.left_shift(1, rel & 7)
+    word_iota = jnp.arange(words, dtype=jnp.int32)
+    packed = jnp.sum(
+        jnp.where(word[:, :, None] == word_iota[None, None, :], bit[:, :, None], 0), axis=1
+    )
+    feature_iota = jnp.arange(feat_block, dtype=jnp.int32)
+    spread = (word_iota[:, None] == (feature_iota // 8)[None, :]).astype(jnp.bfloat16)
+    wide = jnp.dot(
+        packed.astype(jnp.float32).astype(jnp.bfloat16), spread, preferred_element_type=jnp.float32
+    ).astype(jnp.int32)
+    return (jnp.right_shift(wide, (feature_iota & 7)[None, :]) & 1).astype(jnp.bfloat16)
+
+
+def gathered_plan(activations, block_lists, top_positions, enc_weight, enc_bias, dec_weight, dec_bias):
+    feat_block = enc_weight.shape[1]
+    ids = global_ids(block_lists, top_positions, feat_block)
+    all_ids = lax.all_gather(ids, GROUP, axis=0, tiled=True)
+    all_x = lax.all_gather(activations, GROUP, axis=0, tiled=True)
+    mask = select_mask(all_ids - lax.axis_index(GROUP) * feat_block, feat_block)
+    pre_acts = jnp.dot(all_x, enc_weight, preferred_element_type=jnp.float32) + enc_bias
+    code_vals = jnp.where(mask > 0, pre_acts, 0.0).astype(jnp.bfloat16)
+    partial_value = jnp.dot(code_vals, dec_weight, preferred_element_type=jnp.float32).astype(
+        jnp.bfloat16
+    )
+    summed = lax.psum_scatter(partial_value, GROUP, scatter_dimension=0, tiled=True)
+    residual = (
+        summed.astype(jnp.float32) + dec_bias - activations.astype(jnp.float32)
+    ).astype(jnp.bfloat16)
+    all_err = lax.all_gather(residual, GROUP, axis=0, tiled=True)
+    grad_codes = lax.dot_general(
+        all_err, dec_weight, (((1,), (1,)), ((), ())), preferred_element_type=jnp.float32
+    )
+    grad_pre = jnp.where(mask > 0, grad_codes, 0.0).astype(jnp.bfloat16)
+    enc_grad = lax.dot_general(
+        all_x, grad_pre, (((0,), (0,)), ((), ())), preferred_element_type=jnp.float32
+    ).astype(jnp.bfloat16)
+    raw_grad = lax.dot_general(
+        code_vals, all_err, (((0,), (0,)), ((), ())), preferred_element_type=jnp.float32
+    )
+    dec_float = dec_weight.astype(jnp.float32)
+    along_coef = jnp.sum(raw_grad * dec_float, axis=1) / (
+        jnp.sum(dec_float * dec_float, axis=1) + 1e-06
+    )
+    dec_grad = (raw_grad - along_coef[:, None] * dec_float).astype(jnp.bfloat16)
+    return (enc_grad, dec_grad)
+
+
+def on_device(activations, block_lists, top_positions, *weights):
+    owner_count = lax.axis_size(GROUP)
+    pairs = activations.shape[0] * block_lists.shape[1]
+    gathered = owner_count * activations.shape[0]
+    if gathered <= 4 * pairs:
+        return gathered_plan(activations, block_lists, top_positions, *weights)
+    return routed_plan(activations, block_lists, top_positions, *weights)
+
+
 def solution(mesh):
     placed = (
         P(("grp", "tok", "feat"), None),

time: 387 us -> 425 us (1.098)
  waiting for transfers between devices: 66.5 us -> 288 us
  blocking collectives: 219 us -> 45.2 us
  other arithmetic: 42.5 us -> 15.5 us
  matrix products: 33.5 us -> 57.1 us
  between operations: 0.9 us -> 13.8 us
  starting transfers between devices: 12.9 us -> 0.12 us
  local copies, waits for them, and re-layouts: 10.8 us -> 5.31 us
    all_to_all x2 -> x0, blocking collectives: 219 us -> none  [the longest x1 110 us: dispatch_errors(): lax.all_to_all(send_err, ('tok', 'feat'), split_axis=0, concat_axis=0, ti...]
    all_gather x0 -> x2, waiting for transfers between devices: none -> 154 us  [the longest x1 100 us: gathered_plan(): all_err = lax.all_gather(residual, GROUP, axis=0, tiled=True)]
    reduce_scatter x0 -> x1, waiting for transfers between devices: none -> 133 us  [gathered_plan(): lax.psum_scatter(partial_value, GROUP, scatter_dimension=0, tiled=True)]
    all_to_all x2 -> x0, waiting for transfers between devices: 66.5 us -> none  [the longest x1 65.9 us: dispatch_rows(): lax.all_to_all(send_x, ('tok', 'feat'), split_axis=0, concat_axis=0, tile...]
    all_gather x0 -> x1, blocking collectives: none -> 45.2 us  [gathered_plan(): all_ids = lax.all_gather(ids, GROUP, axis=0, tiled=True)]
    reduce_or x4 -> x0, other arithmetic: 34.7 us -> none  [on_device(): jnp.any(piece[:, :, None] == feature_iota[None, None, :], axis=1)]
    dot_general x8 -> x5, matrix products: 33.5 us -> 57.1 us  [the longest x1 23.1 us: gathered_plan(): lax.dot_general(all_x, grad_pre, (((0,), (0,)), ((), ())), preferred_elem...]
    all_to_all x2 -> x0, starting transfers between devices: 12.9 us -> none  [the longest x1 7.39 us: dispatch_rows(): lax.all_to_all(send_rel, ('tok', 'feat'), split_axis=0, concat_axis=0, ti...]
  transfers between devices with their start and end apart: 2 -> 3, of which waited for: 2 -> 3; matrix products, arithmetic and copies ran while one was open for 12% -> 3% of each run, Pallas kernels for 0% -> 0%
where the time goes in v1:
time: 425 us
  waiting for transfers between devices  288 us (68%)
  matrix products  57.1 us (13%)
  blocking collectives  45.2 us (11%)
  other arithmetic  15.5 us (4%)
  between operations  13.8 us (3%)
  local copies, waits for them, and re-layouts  5.31 us (1%)
    reduce_scatter x1, waiting for transfers between devices, gathered_plan(): lax.psum_scatter(partial_value, GROUP, scatter_dimension=0, tiled=True)  133 us
    all_gather x1, waiting for transfers between devices, gathered_plan(): all_err = lax.all_gather(residual, GROUP, axis=0, tiled=True)  100 us
    all_gather x1, waiting for transfers between devices, gathered_plan(): all_x = lax.all_gather(activations, GROUP, axis=0, tiled=True)  54.2 us
    all_gather x1, blocking collectives, gathered_plan(): all_ids = lax.all_gather(ids, GROUP, axis=0, tiled=True)  45.2 us
    dot_general x1, matrix products, gathered_plan(): lax.dot_general(all_x, grad_pre, (((0,), (0,)), ((), ())), preferred_elem...  23.1 us
    dot_general x1, matrix products, gathered_plan(): lax.dot_general(code_vals, all_err, (((0,), (0,)), ((), ())), preferred_e...  11.7 us
    dot_general x1, matrix products, gathered_plan(): jnp.dot(all_x, enc_weight, preferred_element_type=jnp.float32) + enc_bias  10.1 us
    dot_general x1, matrix products, gathered_plan(): jnp.dot(code_vals, dec_weight, preferred_element_type=jnp.float32)  9.73 us
  transfers between devices with their start and end apart: 3, of which 3 were waited for; matrix products, arithmetic and copies ran while one was open for 3% of the time, Pallas kernels for 0%

profile of v1, /device:TPU:0, one launch (start us, length us, event | category | flops | bytes accessed | tf_op | source)
XLA Modules:
  0.0 425.1 jit_solution(17819520309938272814)
XLA Ops:
  7.2 0.0 all-gather.3.cloned.1.call-start
  7.2 0.7 all-gather.3.cloned.1.call-update
  7.9 0.0 reduce-scatter.2.cloned.1.call-start
  8.0 0.9 copy.20
  8.9 0.2 slice_reduce_fusion.3
  9.2 0.8 fusion.11
  10.0 45.2 %all_gather.9 = s32[2048,64]{0,1:T(8,128)S(1)} all-gather(s32[128,64]{0,1:T(8,128)S(1)} %fusion.11), channel_id=1, replica_groups=mesh['grp'=2,'tok'=4,'feat'=4] {'tok','feat'}, dimensions={0}, use_global_device_ids=true | all-gather | bytes 557056 | tf_op jit(solution)/shard_map/all_gather | solution.py:142
  55.2 0.4 fusion.8
  55.6 8.9 %select_reduce_fusion = s32[2048,64]{0,1:T(8,128)S(1)} fusion(s32[2048,64]{0,1:T(8,128)S(1)} %get-tuple-element.17, s32[2048,64]{0,1:T(8,128)S(1)} %get-tuple-element.16), kind=kLoop, calls=%fused_computation | loop fusion | flops 25034752 | bytes 1572864 | tf_op jit(solution)/shard_map/reduce_sum | solution.py:128
  64.6 2.5 fusion.5
  67.0 54.2 %all-gather.3.cloned.1.call-done = bf16[2048,3072]{1,0:T(8,128)(2,1)} async-done(((bf16[128,3072]{1,0:T(8,128)(2,1)}), bf16[2048,3072]{1,0:T(8,128)(2,1)}) %all-gather.3.cloned.1.call-update) | async-done | bytes 12582928 | tf_op jit(solution)/shard_map/all_gather | solution.py:143
  121.2 10.1 %select_convert_fusion.1 = bf16[2048,512]{1,0:T(8,128)(2,1)S(1)} fusion(pred[2048,512]{1,0:T(32,128)(4,1)} %fusion.5, bf16[2048,3072]{1,0:T(8,128)(2,1)} %all-gather.3.cloned.1.call-done, bf16[3072,512]{1,0:T(8,128)(2,1)S(1)} %copy-done, f32[512]{0:T(512)S(1)} %copy-done.6), kind=kOutput, calls=%fused_computation.12 | convolution fusion | flops 6445596672 | bytes 18876416 | tf_op jit(solution)/shard_map/dot_general | solution.py:145
  131.3 1.3 copy-done.7
  132.6 9.7 %convolution_convert_fusion = bf16[2048,3072]{1,0:T(8,128)(2,1)} fusion(bf16[2048,512]{1,0:T(8,128)(2,1)S(1)} %select_convert_fusion.1, bf16[512,3072]{1,0:T(8,128)(2,1)S(1)} %copy-done.3), kind=kOutput, calls=%fused_computation.2 | convolution fusion | flops 6448742400 | bytes 17825792 | tf_op jit(solution)/shard_map/dot_general | solution.py:147
  142.4 0.0 reduce-scatter.2.cloned.1.call-update
  142.4 0.0 all-gather.5.cloned.1.call-start
  142.5 133.0 %reduce-scatter.2.cloned.1.call-done = bf16[128,3072]{1,0:T(8,128)(2,1)} async-done(((bf16[2048,3072]{1,0:T(8,128)(2,1)}), bf16[128,3072]{1,0:T(8,128)(2,1)}) %reduce-scatter.2.cloned.1.call-update) | async-done | bytes 786448 | tf_op jit(solution)/shard_map/reduce_scatter | solution.py:150
  275.5 2.3 subtract_convert_fusion
  277.8 0.0 all-gather.5.cloned.1.call-update
  277.8 100.1 %all-gather.5.cloned.1.call-done = bf16[2048,3072]{1,0:T(8,128)(2,1)} async-done(((bf16[128,3072]{1,0:T(8,128)(2,1)}), bf16[2048,3072]{1,0:T(8,128)(2,1)}) %all-gather.5.cloned.1.call-update) | async-done | bytes 12582928 | tf_op jit(solution)/shard_map/all_gather | solution.py:154
  377.9 23.1 %fusion.4 = bf16[3072,512]{0,1:T(8,128)(2,1)S(1)} fusion(bf16[2048,3072]{1,0:T(8,128)(2,1)} %all-gather.3.cloned.1.call-done, pred[2048,512]{1,0:T(32,128)(4,1)} %fusion.5, bf16[2048,3072]{1,0:T(8,128)(2,1)} %all-gather.5.cloned.1.call-done, bf16[512,3072]{1,0:T(8,128)(2,1)} %param.12), kind=kOutput, calls=%fused_computation.14 | convolution fusion | flops 12888571904 | bytes 32505856 | tf_op jit(solution)/shard_map/dot_general | solution.py:159
  401.0 2.8 copy.21
  403.8 11.7 %fusion.1 = (f32[512]{0:T(512)S(1)}, f32[512]{0:T(512)S(1)}, f32[512,3072]{1,0:T(8,128)S(1)}) fusion(bf16[512,3072]{1,0:T(8,128)(2,1)} %param.12, bf16[2048,512]{1,0:T(8,128)(2,1)} %copy-done.7, bf16[2048,3072]{1,0:T(8,128)(2,1)} %all-gather.5.cloned.1.call-done), kind=kOutput, calls=%fused_computation.7 | convolution fusion | flops 6450314240 | bytes 24121344 | tf_op jit(solution)/shard_map/dot_general | solution.py:162
  415.5 3.1 fusion.3
  (18 shorter events, 0.1 us)
Async XLA Ops:
  7.2 114.0 %copy-start = (bf16[3072,512]{1,0:T(8,128)(2,1)S(1)}, bf16[3072,512]{1,0:T(8,128)(2,1)}, u32[]{:S(2)}) copy-start(bf16[3072,512]{1,0:T(8,128)(2,1)} %param.10) | copy-start | bytes 9437188
  7.2 114.0 %all-gather.3.cloned.1.call-start = ((), (), s32[]{:S(2)}) async-start(), calls=%async_computation.1 | async-start | bytes 13369344 | tf_op jit(solution)/shard_map/all_gather | solution.py:143
  7.9 267.6 %reduce-scatter.2.cloned.1.call-start = ((), (), s32[]{:S(2)}) async-start(), calls=%async_computation.2 | async-start | bytes 13369344 | tf_op jit(solution)/shard_map/reduce_scatter | solution.py:150
  64.5 56.7 %copy-start.6 = (f32[512]{0:T(512)S(1)}, f32[512]{0:T(512)}, u32[]{:S(2)}) copy-start(f32[512]{0:T(512)} %param.11) | copy-start | bytes 6148
  121.2 11.4 %copy-start.3 = (bf16[512,3072]{1,0:T(8,128)(2,1)S(1)}, bf16[512,3072]{1,0:T(8,128)(2,1)}, u32[]{:S(2)}) copy-start(bf16[512,3072]{1,0:T(8,128)(2,1)} %param.12) | copy-start | bytes 9437188
  131.3 1.3 copy-start.7
  142.4 133.1 %copy-start.2 = (bf16[128,3072]{1,0:T(8,128)(2,1)S(1)}, bf16[128,3072]{1,0:T(8,128)(2,1)}, u32[]{:S(2)}) copy-start(bf16[128,3072]{1,0:T(8,128)(2,1)} %param.7) | copy-start | bytes 2359300
  142.4 133.1 %copy-start.5 = (f32[3072]{0:T(1024)S(1)}, f32[3072]{0:T(1024)}, u32[]{:S(2)}) copy-start(f32[3072]{0:T(1024)} %param.13) | copy-start | bytes 36868
  142.4 235.5 %all-gather.5.cloned.1.call-start = ((), (), s32[]{:S(2)}) async-start(), calls=%async_computation.3 | async-start | bytes 13369344 | tf_op jit(solution)/shard_map/all_gather | solution.py:154
  403.8 11.7 %copy-start.4 = (bf16[512,3072]{1,0:T(8,128)(2,1)S(1)}, bf16[512,3072]{1,0:T(8,128)(2,1)}, u32[]{:S(2)}) copy-start(bf16[512,3072]{1,0:T(8,128)(2,1)} %param.12) | copy-start | bytes 9437188
  415.5 3.1 copy-start.1
Sparse Core Ops, SparseCore 0:
  10.3 110.8 all-gather.2
  142.5 132.9 reduce-scatter.1
  277.9 99.8 all-gather.4
